TPU v7x, 512 devices: a whole 4x8x8 slice. The times are simulated.
512 devices in a mesh: seq: 32 (over y, x), head: 16 (over z, core).
Axes of the slice: x: 4, y: 8, z: 8, core: 2. Of those that a mesh axis runs over, the one named last changes fastest.
Arguments:
- x_input: bfloat16 [4096, 16384], P('seq', 'head'), may hold values from -6 to 6
- z_input: bfloat16 [4096, 16384], P('seq', 'head'), may hold values from -52 to 52
- bc_input: bfloat16 [2, 4096, 128], P(None, 'seq'), may hold values from -2.09375 to 2.09375
- dt_raw: float32 [128, 4096], P('head', 'seq'), may hold values from -1.5 to 4.5
- dt_bias: float32 [128], P('head'), may hold values from -4.2 to 0.3
- a_log: float32 [128], P('head')
- d_skip: float32 [128], P('head'), may hold values from 0.5 to 1.5
- conv_x: float32 [4, 16384], P(None, 'head'), may hold values from -3 to 3
- convolution_bc_taps: float32 [2, 4, 128], replicated, may hold values from -3 to 3
- rescale_factor: float32 [16384], P('head'), may hold values from 0.5 to 1.5
- grad_out: bfloat16 [4096, 16384], P('seq', 'head'), may hold values from -40 to 40
Outputs:
- grad_x: bfloat16 [4096, 16384], P('seq', 'head')
- grad_z: bfloat16 [4096, 16384], P('seq', 'head')
- grad_bc: bfloat16 [2, 4096, 128], P(None, ('seq', 'head'))
- grad_dt: float32 [128, 4096], P('head', 'seq')
All inputs are finite; a program needn't handle non-finite values.
Results may differ from a plain program's by a relative error of at most 0.0086.
Values may be sent and summed in bfloat16 or wider, within the bound.
A program may use at most 64 MiB of HBM per device.

v0:
```python
import jax
import jax.numpy as jnp
from jax import lax
from jax.sharding import PartitionSpec as P

INNER = 16384
EPS = 1e-05


def entering(part, axis, combine, identity, reverse):
    count = lax.axis_size(axis)
    place = lax.axis_index(axis)
    ahead = count - 1 - place if reverse else place
    gathered = jax.tree.map(lambda a: lax.all_gather(a, axis), part)
    state = jax.tree.map(lambda a, e: jnp.zeros_like(a) + jnp.asarray(e, a.dtype), part, identity)

    def one(hop, state):
        source = count - 1 - hop if reverse else hop
        return combine(
            state, jax.tree.map(lambda a: lax.dynamic_index_in_dim(a, source, 0, False), gathered)
        )

    return lax.fori_loop(0, ahead, one, state)


def passed_along(block, axis, distance):
    devices = range(lax.axis_size(axis))
    route = [(i - distance, i) for i in devices if i - distance in devices]
    return lax.ppermute(block, axis, route)


def silu_grad(value):
    sigma = jax.nn.sigmoid(value)
    return sigma * (1.0 + value * (1.0 - sigma))


def conv_rows(extended, weight_matrix):
    length = extended.shape[-2] - 3
    summed = weight_matrix[..., 0, :][..., None, :] * extended[..., 0:length, :]
    for offset in range(1, 4):
        summed = (
            summed
            + weight_matrix[..., offset, :][..., None, :]
            * extended[..., offset : offset + length, :]
        )
    return summed


def conv_back(extended, weight_matrix):
    length = extended.shape[-2] - 3
    summed = weight_matrix[..., 0, :][..., None, :] * extended[..., 3 : 3 + length, :]
    for offset in range(1, 4):
        summed = (
            summed
            + weight_matrix[..., offset, :][..., None, :]
            * extended[..., 3 - offset : 3 - offset + length, :]
        )
    return summed


def decay_of(cumul, causal):
    between = cumul[:, None] - cumul[None, :]
    return jnp.where(causal, jnp.exp(jnp.minimum(between, 0.0)), 0.0)


def weighted_rows(trailing_decay, step_size, b_rows):
    return ((trailing_decay * step_size)[:, None] * b_rows.astype(jnp.float32)).astype(jnp.bfloat16)


def head_forward(cumul, step_size, gram_matrix, x_head, state_low, c_rows, skip_gain, causal):
    decay_matrix = decay_of(cumul, causal)
    mixer_low = (gram_matrix * decay_matrix * step_size[None, :]).astype(jnp.bfloat16)
    intra_out = jnp.dot(mixer_low, x_head, preferred_element_type=jnp.float32)
    handed_forward = jnp.dot(c_rows, state_low, preferred_element_type=jnp.float32)
    return (
        intra_out
        + jnp.exp(cumul)[:, None] * handed_forward
        + skip_gain * x_head.astype(jnp.float32)
    )


def head_backward(
    cumul,
    step_size,
    gram_matrix,
    x_head,
    grad_head,
    state_low,
    state_exact,
    out_low,
    out_exact,
    b_rows,
    c_rows,
    skip_gain,
    decay_rate,
    causal,
):
    decay_matrix = decay_of(cumul, causal)
    mixer_low = (gram_matrix * decay_matrix * step_size[None, :]).astype(jnp.bfloat16)
    grad_mix = jnp.dot(grad_head, x_head.T, preferred_element_type=jnp.float32)
    decayed_grad = grad_mix * decay_matrix
    weighted_grad = decayed_grad * step_size[None, :]
    gram_grad = weighted_grad * gram_matrix
    lifted = jnp.exp(cumul)
    handed_forward = jnp.dot(c_rows, state_low, preferred_element_type=jnp.float32)
    reached = jnp.dot(x_head, out_low.T, preferred_element_type=jnp.float32)
    trailing_decay = jnp.exp(cumul[-1] - cumul)
    inner_b = jnp.sum(b_rows.astype(jnp.float32) * reached, axis=1)
    state_term = trailing_decay * step_size * inner_b
    grad_cumul = jnp.sum(gram_grad, axis=1) - jnp.sum(gram_grad, axis=0)
    grad_cumul = (
        grad_cumul
        + lifted * jnp.sum(grad_head.astype(jnp.float32) * handed_forward, axis=1)
        - state_term
    )
    end_grad = jnp.sum(state_term) + jnp.exp(cumul[-1]) * jnp.sum(out_exact * state_exact)
    grad_cumul = grad_cumul.at[-1].add(end_grad)
    grad_log = jnp.cumsum(grad_cumul[::-1])[::-1]
    grad_step = (
        jnp.sum(decayed_grad * gram_matrix, axis=0)
        + trailing_decay * inner_b
        + decay_rate * grad_log
    )
    weighted_b = weighted_rows(trailing_decay, step_size, b_rows)
    grad_x = jnp.dot(mixer_low.T, grad_head, preferred_element_type=jnp.float32)
    grad_x = (
        grad_x
        + skip_gain * grad_head.astype(jnp.float32)
        + jnp.dot(weighted_b, out_low, preferred_element_type=jnp.float32)
    )
    grad_c = lifted[:, None] * jnp.dot(grad_head, state_low.T, preferred_element_type=jnp.float32)
    grad_b = (trailing_decay * step_size)[:, None] * reached
    return (grad_x, grad_step, grad_c, grad_b, weighted_grad)


def block_prep(x_rows, b_rows, step_size, decay_rate):
    length = x_rows.shape[0]
    head_count = step_size.shape[0]
    cumul = jnp.cumsum(decay_rate[:, None] * step_size, axis=1)
    trailing_decay = jnp.exp(cumul[:, -1:] - cumul)
    x_heads = jnp.moveaxis(x_rows.reshape(length, head_count, -1), 1, 0)

    def one_head(head_items):
        weighted_b = weighted_rows(head_items[0], head_items[1], b_rows)
        return jnp.dot(weighted_b.T, head_items[2], preferred_element_type=jnp.float32)

    local_state = lax.map(one_head, (trailing_decay, step_size, x_heads))
    return (cumul, x_heads, local_state)


def block_mix(cumul, step_size, gram_matrix, x_heads, state_low, c_rows, skip_gain, causal):

    def one_head(head_items):
        return head_forward(
            head_items[0],
            head_items[1],
            gram_matrix,
            head_items[2],
            head_items[3],
            c_rows,
            head_items[4],
            causal,
        )

    outputs = lax.map(one_head, (cumul, step_size, x_heads, state_low, skip_gain))
    return jnp.moveaxis(outputs, 0, 1).reshape(outputs.shape[1], -1)


def carry_grad(cumul, c_rows, grad_heads):

    def one_head(head_items):
        lifted_c = (jnp.exp(head_items[0])[:, None] * c_rows.astype(jnp.float32)).astype(
            jnp.bfloat16
        )
        return jnp.dot(lifted_c.T, head_items[1], preferred_element_type=jnp.float32)

    return lax.map(one_head, (cumul, grad_heads))


def block_back(
    cumul,
    step_size,
    gram_matrix,
    x_heads,
    grad_heads,
    state_exact,
    out_exact,
    b_rows,
    c_rows,
    skip_gain,
    decay_rate,
    causal,
):
    length = b_rows.shape[0]
    nstate = b_rows.shape[1]
    state_low = state_exact.astype(jnp.bfloat16)
    out_low = out_exact.astype(jnp.bfloat16)

    def one_head(running, head_items):
        (
            cumulative_head,
            step_head,
            x_head,
            grad_head,
            low_in,
            exact_in,
            low_out,
            exact_out,
            skip_head,
            rate_head,
        ) = head_items
        grad_x, grad_step, grad_c, grad_b, weighted_grad = head_backward(
            cumulative_head,
            step_head,
            gram_matrix,
            x_head,
            grad_head,
            low_in,
            exact_in,
            low_out,
            exact_out,
            b_rows,
            c_rows,
            skip_head,
            rate_head,
            causal,
        )
        return (
            (running[0] + weighted_grad, running[1] + grad_c, running[2] + grad_b),
            (grad_x, grad_step),
        )

    initial = (
        jnp.zeros((length, length), jnp.float32),
        jnp.zeros((length, nstate), jnp.float32),
        jnp.zeros((length, nstate), jnp.float32),
    )
    (grad_sum, c_sum, b_sum), (grad_xs, grad_steps) = lax.scan(
        one_head,
        initial,
        (
            cumul,
            step_size,
            x_heads,
            grad_heads,
            state_low,
            state_exact,
            out_low,
            out_exact,
            skip_gain,
            decay_rate,
        ),
    )
    grad_c = c_sum + jnp.dot(grad_sum, b_rows.astype(jnp.float32), precision=lax.Precision.HIGHEST)
    grad_b = b_sum + jnp.dot(
        grad_sum.T, c_rows.astype(jnp.float32), precision=lax.Precision.HIGHEST
    )
    grad_x = jnp.moveaxis(grad_xs, 0, 1).reshape(length, -1)
    return (grad_x, jnp.stack([grad_b, grad_c]), grad_steps)


def pass_states(totals, states, reverse):
    factor = jnp.exp(totals)[:, None, None]

    def combine(earlier, latter):
        return (earlier[0] * latter[0], latter[0] * earlier[1] + latter[1])

    result = entering(
        (factor, states), "seq", combine, (jnp.ones_like(factor), jnp.zeros_like(states)), reverse
    )
    return result[1]


def shards(
    x_input,
    z_input,
    bc_input,
    dt_raw,
    dt_bias,
    a_log,
    d_skip,
    conv_x,
    convolution_bc_taps,
    rescale_factor,
    grad_out,
):
    length = x_input.shape[0]
    head_count = dt_raw.shape[0]
    decay_rate = -jnp.exp(a_log)
    step_size = jax.nn.softplus(dt_raw + dt_bias[:, None])
    causal = jnp.tril(jnp.ones((length, length), dtype=bool))
    rows_prior = passed_along((x_input[length - 3 :], bc_input[:, length - 3 :]), "seq", 1)
    x_ext = jnp.concatenate([rows_prior[0], x_input], axis=0)
    bc_ext = jnp.concatenate([rows_prior[1], bc_input], axis=1)
    x_pre = conv_rows(x_ext.astype(jnp.float32), conv_x)
    bc_pre = conv_rows(bc_ext.astype(jnp.float32), convolution_bc_taps)
    x_rows = jax.nn.silu(x_pre).astype(jnp.bfloat16)
    bc_rows = jax.nn.silu(bc_pre).astype(jnp.bfloat16)
    gram_matrix = jnp.dot(bc_rows[1], bc_rows[0].T, preferred_element_type=jnp.float32)
    cumul, x_heads, local_state = block_prep(x_rows, bc_rows[0], step_size, decay_rate)
    totals = cumul[:, -1]
    state_exact = pass_states(totals, local_state, False)
    mixed_out = block_mix(
        cumul,
        step_size,
        gram_matrix,
        x_heads,
        state_exact.astype(jnp.bfloat16),
        bc_rows[1],
        d_skip,
        causal,
    )
    z_rows = z_input.astype(jnp.float32)
    gate_value = jax.nn.silu(z_rows)
    gated = mixed_out * gate_value
    square_sum = lax.psum(jnp.sum(gated * gated, axis=1), "head")
    inv_rms = lax.rsqrt(square_sum / INNER + EPS)
    normed = gated * inv_rms[:, None]
    scaled = grad_out.astype(jnp.float32) * rescale_factor
    product_sum = lax.psum(jnp.sum(scaled * normed, axis=1), "head")
    mean_dot = product_sum / INNER
    grad_gated = inv_rms[:, None] * (scaled - normed * mean_dot[:, None])
    grad_z = (grad_gated * mixed_out * silu_grad(z_rows)).astype(jnp.bfloat16)
    grad_mixed = (grad_gated * gate_value).astype(jnp.bfloat16)
    grad_heads = jnp.moveaxis(grad_mixed.reshape(length, head_count, -1), 1, 0)
    state_grad = carry_grad(cumul, bc_rows[1], grad_heads)
    out_exact = pass_states(totals, state_grad, True)
    grad_x_rows, grad_bc_rows, grad_steps = block_back(
        cumul,
        step_size,
        gram_matrix,
        x_heads,
        grad_heads,
        state_exact,
        out_exact,
        bc_rows[0],
        bc_rows[1],
        d_skip,
        decay_rate,
        causal,
    )
    grad_x_pre = grad_x_rows * silu_grad(x_pre)
    row_share = length // lax.axis_size("head")
    first_row = lax.axis_index("head") * row_share
    grad_bc_all = lax.psum(grad_bc_rows, "head")
    grad_bc_pre = grad_bc_all * silu_grad(bc_pre)
    rows_next = passed_along((grad_x_pre[:3], grad_bc_pre[:, :3]), "seq", -1)
    grad_x = conv_back(jnp.concatenate([grad_x_pre, rows_next[0]], axis=0), conv_x).astype(
        jnp.bfloat16
    )
    grad_bc_full = conv_back(
        jnp.concatenate([grad_bc_pre, rows_next[1]], axis=1), convolution_bc_taps
    )
    grad_bc = lax.dynamic_slice_in_dim(grad_bc_full, first_row, row_share, 1).astype(jnp.bfloat16)
    grad_dt = grad_steps * jax.nn.sigmoid(dt_raw + dt_bias[:, None])
    return (grad_x, grad_z, grad_bc, grad_dt)


def solution(mesh):
    return jax.shard_map(
        shards,
        mesh=mesh,
        in_specs=(
            P("seq", "head"),
            P("seq", "head"),
            P(None, "seq", None),
            P("head", "seq"),
            P("head"),
            P("head"),
            P("head"),
            P(None, "head"),
            P(),
            P("head"),
            P("seq", "head"),
        ),
        out_specs=(
            P("seq", "head"),
            P("seq", "head"),
            P(None, ("seq", "head"), None),
            P("head", "seq"),
        ),
        check_vma=False,
    )
```

profile of v0, /device:TPU:30, one launch (start us, length us, event | category | flops | bytes accessed | tf_op | source)
XLA Modules:
  0.0 696.2 jit_solution(10006820068092498792)
XLA Ops:
  8.0 4.6 collective-permute-start
  13.3 3.4 collective-permute-start.1
  23.6 2.3 while.85
  26.8 1.3 dynamic-slice.7
  28.9 69.7 %all-reduce = f32[256]{0:T(256)S(1)} all-reduce(f32[256]{0:T(256)S(1)} %dynamic-update-slice.5), channel_id=2, replica_groups=mesh['seq'=32,'head'=16] {'seq'}, use_global_device_ids=true, to_apply=%add | all-reduce | flops 256 | bytes 2048
  98.9 73.7 %all-gather.6.cloned.1.call-done = f32[256,128,128]{2,1,0:T(8,128)} async-done(((f32[8,128,128]{2,1,0:T(8,128)}), f32[256,128,128]{2,1,0:T(8,128)}) %all-gather.6.cloned.1.call-update) | async-done | bytes 16777232 | tf_op jit(solution)/shard_map/all_gather | solution.py:14
  172.6 18.5 %while.86 = (s32[]{:T(128)}, f32[8,128,128]{2,1,0:T(8,128)S(1)}, s32[]{:T(128)}, f32[32,8,1,1]{1,3,2,0:T(1,128)S(1)}, f32[32,8,128,128]{3,2,1,0:T(8,128)}) while((s32[]{:T(128)}, f32[8,128,128]{2,1,0:T(8,128)S(1)}, s32[]{:T(128)}, f32[32,8,1,1]{1,3,2,0:T(1,128)S(1)}, f32[32,8,128,128]{3,2,1,0:T(8,128)}) %tuple.221), condition=%wide.region_4.5_spmd.clone, body=%wide.region_3.4_spmd.sunk.clone | while | flops 262149 | bytes 1573063 | solution.py:23
  172.7 1.2 bitcast_add_fusion.6
  175.2 1.2 bitcast_add_fusion.6
  177.6 1.2 bitcast_add_fusion.6
  180.1 1.2 bitcast_add_fusion.6
  191.3 13.1 %while.89 = (s32[]{:T(128)}, f32[8,128,128]{2,1,0:T(8,128)S(1)}, f32[8,128]{1,0:T(8,128)S(1)}, f32[128,128]{1,0:T(8,128)S(1)}, f32[8,128]{1,0:T(8,128)S(1)}, /*i...) while((s32[]{:T(128)}, f32[8,128,128]{2,1,0:T(8,128)S(1)}, ...), condition=%wide.region_6.7_spmd.clone.clone, body=%wide.region_5.6_spmd.clone.sunk.clone | while | flops 8585218 | bytes 399477 | solution.py:165
  204.7 26.9 %psum.21 = f32[128]{0:T(128)S(1)} all-reduce(f32[128]{0:T(128)S(1)} %multiply_reduce_fusion.4), channel_id=1, replica_groups=mesh['seq'=32,'head'=16] {'head'}, use_global_device_ids=true, to_apply=%region_8.9 | all-reduce | flops 128 | bytes 1024 | tf_op jit(solution)/shard_map/psum | solution.py:316
  232.0 23.5 %psum.22 = f32[128]{0:T(128)S(1)} all-reduce(f32[128]{0:T(128)S(1)} %multiply_reduce_fusion.3), channel_id=1, replica_groups=mesh['seq'=32,'head'=16] {'head'}, use_global_device_ids=true, to_apply=%region_10.11 | all-reduce | flops 128 | bytes 1024 | tf_op jit(solution)/shard_map/psum | solution.py:320
  256.7 2.3 while.87
  260.1 157.1 %all-gather.8.cloned.1.call-done = f32[256,128,128]{2,1,0:T(8,128)} async-done(((f32[8,128,128]{2,1,0:T(8,128)}), f32[256,128,128]{2,1,0:T(8,128)}) %all-gather.8.cloned.1.call-update) | async-done | bytes 16777232 | tf_op jit(solution)/shard_map/all_gather | solution.py:14
  417.2 19.7 %while.88 = (s32[]{:T(128)}, f32[8,128,128]{2,1,0:T(8,128)S(1)}, s32[]{:T(128)}, f32[32,8,1,1]{1,3,2,0:T(1,128)S(1)}, f32[32,8,128,128]{3,2,1,0:T(8,128)}) while((s32[]{:T(128)}, f32[8,128,128]{2,1,0:T(8,128)S(1)}, s32[]{:T(128)}, f32[32,8,1,1]{1,3,2,0:T(1,128)S(1)}, f32[32,8,128,128]{3,2,1,0:T(8,128)}) %tuple.222), condition=%wide.region_14.15_spmd.clone, body=%wide.region_13.14_spmd.sunk.clone | while | flops 262150 | bytes 1573075 | solution.py:23
  437.8 112.0 %while.90 = (s32[]{:T(128)}, f32[128,128]{1,0:T(8,128)S(1)}, f32[128,128]{1,0:T(8,128)S(1)}, f32[128,128]{0,1:T(8,128)S(1)}, f32[8,128,128]{2,1,0:T(8,128)S(1)},...) while((s32[]{:T(128)}, f32[128,128]{1,0:T(8,128)S(1)}, ...), condition=%wide.region_24.25_spmd.clone.clone, body=%wide.region_15.24_spmd.clone.sunk.clone | while | flops 25854976 | bytes 1473321 | solution.py:238
  439.3 1.3 multiply_reduce_fusion.9
  444.6 1.3 dynamic_slice.354
  445.9 1.3 add_bitcast_fusion.3
  447.1 1.3 dynamic_update_slice.44
  448.4 1.2 dynamic_slice.353
  453.3 1.3 multiply_reduce_fusion.9
  458.6 1.3 dynamic_slice.354
  459.9 1.3 add_bitcast_fusion.3
  461.1 1.3 dynamic_update_slice.44
  462.4 1.2 dynamic_slice.353
  467.3 1.3 multiply_reduce_fusion.9
  472.6 1.3 dynamic_slice.354
  473.9 1.3 add_bitcast_fusion.3
  475.1 1.3 dynamic_update_slice.44
  476.4 1.2 dynamic_slice.353
  481.3 1.3 multiply_reduce_fusion.9
  486.6 1.3 dynamic_slice.354
  487.9 1.3 add_bitcast_fusion.3
  489.1 1.3 dynamic_update_slice.44
  490.4 1.2 dynamic_slice.353
  495.3 1.3 multiply_reduce_fusion.9
  500.6 1.3 dynamic_slice.354
  501.8 1.3 add_bitcast_fusion.3
  503.1 1.3 dynamic_update_slice.44
  504.4 1.2 dynamic_slice.353
  509.3 1.3 multiply_reduce_fusion.9
  514.6 1.3 dynamic_slice.354
  515.8 1.3 add_bitcast_fusion.3
  517.1 1.3 dynamic_update_slice.44
  518.4 1.2 dynamic_slice.353
  523.3 1.3 multiply_reduce_fusion.9
  528.6 1.3 dynamic_slice.354
  529.8 1.3 add_bitcast_fusion.3
  531.1 1.3 dynamic_update_slice.44
  532.4 1.2 dynamic_slice.353
  537.3 1.3 multiply_reduce_fusion.9
  542.6 1.3 dynamic_slice.354
  543.8 1.3 add_bitcast_fusion.3
  545.1 1.3 dynamic_update_slice.44
  546.4 1.2 dynamic_slice.353
  551.2 4.3 collective-permute-start.2
  555.5 1.4 divide_multiply_fusion
  556.9 3.3 collective-permute-done.2
  561.1 118.1 %all-reduce.3.cloned.1.call-done = f32[2,128,128]{2,1,0:T(8,128)} async-done(((f32[2,128,128]{2,1,0:T(8,128)}), f32[2,128,128]{2,1,0:T(8,128)}) %all-reduce.3.cloned.1.call-update) | async-done | bytes 131088 | tf_op jit(solution)/shard_map/psum | solution.py:345
  680.2 2.8 collective-permute-start.3
  683.0 6.0 collective-permute-done.3
  (340 shorter events, 110.9 us)
Async XLA Ops:
  7.2 184.1 %copy-start.7 = (f32[8]{0:T(128)S(1)}, f32[8]{0:T(128)}, u32[]{:S(2)}) copy-start(f32[8]{0:T(128)} %param.31) | copy-start | bytes 100
  7.2 197.3 %copy-start = (bf16[128,1024]{1,0:T(8,128)(2,1)S(1)}, bf16[128,1024]{1,0:T(8,128)(2,1)}, u32[]{:S(2)}) copy-start(bf16[128,1024]{1,0:T(8,128)(2,1)} %param.26) | copy-start | bytes 786436
  7.2 224.5 %copy-start.4 = (f32[1024]{0:T(1024)S(1)}, f32[1024]{0:T(1024)}, u32[]{:S(2)}) copy-start(f32[1024]{0:T(1024)} %param.34) | copy-start | bytes 12292
  7.2 224.5 %copy-start.3 = (bf16[128,1024]{1,0:T(8,128)(2,1)S(1)}, bf16[128,1024]{1,0:T(8,128)(2,1)}, u32[]{:S(2)}) copy-start(bf16[128,1024]{1,0:T(8,128)(2,1)} %param.35) | copy-start | bytes 786436
  7.2 165.4 %all-gather.6.cloned.1.call-start = ((), (), s32[]{:S(2)}) async-start(), calls=%async_computation.1 | async-start | bytes 17301504 | tf_op jit(solution)/shard_map/all_gather | solution.py:14
  8.0 12.5 %collective-permute-start = (bf16[2,3,128]{2,1,0:T(4,128)(2,1)S(1)}, bf16[2,3,128]{2,1,0:T(4,128)(2,1)S(1)}, u32[]{:S(2)}, u32[]{:S(2)}) collective-permute-start(bf16[2,3,128]{2,1,0:T(4,128)(2,1)S(1)} %slice.125), channel_id=1, source_target_pairs={{0,16},{16,32},{32,48},{48,64},{64,80},{80,96},{96,112},{112,128},... | collective-permute-start | bytes 4616 | tf_op jit(solution)/shard_map/ppermute | solution.py:29
  13.3 8.7 %collective-permute-start.1 = (bf16[3,1024]{1,0:T(4,128)(2,1)S(1)}, bf16[3,1024]{1,0:T(4,128)(2,1)S(1)}, u32[]{:S(2)}, u32[]{:S(2)}) collective-permute-start(bf16[3,1024]{1,0:T(4,128)(2,1)S(1)} %slice.135), channel_id=1, source_target_pairs={{0,16},{16,32},{32,48},{48,64},{64,80},{80,96},{96,112},{112,128},... | collective-permute-start | bytes 18440 | tf_op jit(solution)/shard_map/ppermute | solution.py:29
  18.3 0.8 copy-start.6
  25.9 0.8 copy-start.1
  26.7 390.5 %all-gather.8.cloned.1.call-start = ((), (), s32[]{:S(2)}) async-start(), calls=%async_computation.2 | async-start | bytes 17301504 | tf_op jit(solution)/shard_map/all_gather | solution.py:14
  191.2 364.3 %copy-start.5 = (f32[8,128]{1,0:T(8,128)S(1)}, f32[8,128]{1,0:T(8,128)}, u32[]{:S(2)}) copy-start(f32[8,128]{1,0:T(8,128)} %param.28) | copy-start | bytes 12292
  259.0 0.8 copy-start.2
  259.9 419.3 %all-reduce.3.cloned.1.call-start = ((), (), s32[]{:S(2)}) async-start(), calls=%async_computation | async-start | bytes 262144 | tf_op jit(solution)/shard_map/psum | solution.py:345
  551.2 9.0 %collective-permute-start.2 = (f32[3,1024]{1,0:T(4,128)S(1)}, f32[3,1024]{1,0:T(4,128)S(1)}, u32[]{:S(2)}, u32[]{:S(2)}) collective-permute-start(f32[3,1024]{1,0:T(4,128)S(1)} %slice.164), channel_id=1, source_target_pairs={{16,0},{32,16},{48,32},{64,48},{80,64},{96,80},{112,96},{128,112},... | collective-permute-start | bytes 36872 | tf_op jit(solution)/shard_map/ppermute | solution.py:29
  680.2 8.8 %collective-permute-start.3 = (f32[2,3,128]{2,1,0:T(4,128)S(1)}, f32[2,3,128]{2,1,0:T(4,128)S(1)}, u32[]{:S(2)}, u32[]{:S(2)}) collective-permute-start(f32[2,3,128]{2,1,0:T(4,128)S(1)} %slice.169), channel_id=1, source_target_pairs={{16,0},{32,16},{48,32},{64,48},{80,64},{96,80},{112,96},{128,112},... | collective-permute-start | bytes 9224 | tf_op jit(solution)/shard_map/ppermute | solution.py:29
Sparse Core Ops, SparseCore 0:
  26.8 145.7 all-gather.5
  260.0 157.1 all-gather.7
  551.1 128.0 all-reduce.2
where the time goes:
time: 700 us; the launch traced here: 696 us
  waiting for transfers between devices  358 us (51%)
  blocking collectives  120 us (17%)
  other arithmetic  78.8 us (11%)
  local copies, waits for them, and re-layouts  50.1 us (7%)
  matrix products  40.3 us (6%)
  loops' own time  18.7 us (3%)
  starting transfers between devices  15.2 us (2%)
  between operations  14.8 us (2%)
    all_gather x2, waiting for transfers between devices, entering(): gathered = jax.tree.map(lambda a: lax.all_gather(a, axis), part)  231 us
    psum x1, waiting for transfers between devices, shards(): grad_bc_all = lax.psum(grad_bc_rows, 'head')  118 us
    unnamed x1, blocking collectives  69.7 us
    add x31, other arithmetic, combine(): return (earlier[0] * latter[0], latter[0] * earlier[1] + latter[1])  36.9 us
    psum x1, blocking collectives, shards(): square_sum = lax.psum(jnp.sum(gated * gated, axis=1), 'head')  26.9 us
    dynamic_slice x24, local copies, waits for them, and re-layouts, block_mix(): lax.map(one_head, (cumul, step_size, x_heads, state_low, skip_gain))  24.8 us
    psum x1, blocking collectives, shards(): product_sum = lax.psum(jnp.sum(scaled * normed, axis=1), 'head')  23.5 us
    another operation x1, loops' own time, block_back(): lax.scan(one_head, initial, (cumul, step_size, x_heads, grad_heads, state...  16.9 us
  transfers between devices with their start and end apart: 7, of which 5 were waited for; matrix products, arithmetic and copies ran while one was open for 2% of the time, Pallas kernels for 0%

commit v1 on v0

--- a/solution.py
+++ b/solution.py
@@ -313,7 +313,7 @@
     z_rows = z_input.astype(jnp.float32)
     gate_value = jax.nn.silu(z_rows)
     gated = mixed_out * gate_value
-    square_sum = lax.psum(jnp.sum(gated * gated, axis=1), "head")
+    square_sum = jnp.sum(lax.all_gather(jnp.sum(gated * gated, axis=1), "head"), axis=0)
     inv_rms = lax.rsqrt(square_sum / INNER + EPS)
     normed = gated * inv_rms[:, None]
     scaled = grad_out.astype(jnp.float32) * rescale_factor

time: 700 us -> 693 us (0.990)
  blocking collectives: 120 us -> 112 us
    psum x1 -> x0, blocking collectives: 26.9 us -> none  [shards(): square_sum = lax.psum(jnp.sum(gated * gated, axis=1), 'head')]
    all_gather x0 -> x1, blocking collectives: none -> 18.2 us  [shards(): lax.all_gather(jnp.sum(gated * gated, axis=1), 'head')]
where the time goes in v1:
time: 693 us; the launch traced here: 689 us
  waiting for transfers between devices  359 us (52%)
  blocking collectives  112 us (16%)
  other arithmetic  78.8 us (11%)
  local copies, waits for them, and re-layouts  50.1 us (7%)
  matrix products  40.3 us (6%)
  loops' own time  18.7 us (3%)
  starting transfers between devices  15.2 us (2%)
  between operations  14.8 us (2%)
    all_gather x2, waiting for transfers between devices, entering(): gathered = jax.tree.map(lambda a: lax.all_gather(a, axis), part)  232 us
    psum x1, waiting for transfers between devices, shards(): grad_bc_all = lax.psum(grad_bc_rows, 'head')  118 us
    unnamed x1, blocking collectives  69.7 us
    add x31, other arithmetic, combine(): return (earlier[0] * latter[0], latter[0] * earlier[1] + latter[1])  36.9 us
    dynamic_slice x24, local copies, waits for them, and re-layouts, block_mix(): lax.map(one_head, (cumul, step_size, x_heads, state_low, skip_gain))  24.8 us
    psum x1, blocking collectives, shards(): product_sum = lax.psum(jnp.sum(scaled * normed, axis=1), 'head')  23.8 us
    all_gather x1, blocking collectives, shards(): lax.all_gather(jnp.sum(gated * gated, axis=1), 'head')  18.2 us
    another operation x1, loops' own time, block_back(): lax.scan(one_head, initial, (cumul, step_size, x_heads, grad_heads, state...  16.9 us
  transfers between devices with their start and end apart: 7, of which 5 were waited for; matrix products, arithmetic and copies ran while one was open for 2% of the time, Pallas kernels for 0%

profile of v1, /device:TPU:30, one launch (start us, length us, event | category | flops | bytes accessed | tf_op | source)
XLA Modules:
  0.0 688.6 jit_solution(7793949799260121262)
XLA Ops:
  8.0 4.6 collective-permute-start
  13.3 3.4 collective-permute-start.1
  23.6 2.3 while.85
  26.8 1.3 dynamic-slice.7
  28.9 69.7 %all-reduce = f32[256]{0:T(256)S(1)} all-reduce(f32[256]{0:T(256)S(1)} %dynamic-update-slice.5), channel_id=2, replica_groups=mesh['seq'=32,'head'=16] {'seq'}, use_global_device_ids=true, to_apply=%add | all-reduce | flops 256 | bytes 2048
  98.9 73.7 %all-gather.8.cloned.1.call-done = f32[256,128,128]{2,1,0:T(8,128)} async-done(((f32[8,128,128]{2,1,0:T(8,128)}), f32[256,128,128]{2,1,0:T(8,128)}) %all-gather.8.cloned.1.call-update) | async-done | bytes 16777232 | tf_op jit(solution)/shard_map/all_gather | solution.py:14
  172.6 18.5 %while.86 = (s32[]{:T(128)}, f32[8,128,128]{2,1,0:T(8,128)S(1)}, s32[]{:T(128)}, f32[32,8,1,1]{1,3,2,0:T(1,128)S(1)}, f32[32,8,128,128]{3,2,1,0:T(8,128)}) while((s32[]{:T(128)}, f32[8,128,128]{2,1,0:T(8,128)S(1)}, s32[]{:T(128)}, f32[32,8,1,1]{1,3,2,0:T(1,128)S(1)}, f32[32,8,128,128]{3,2,1,0:T(8,128)}) %tuple.221), condition=%wide.region_4.5_spmd.clone, body=%wide.region_3.4_spmd.sunk.clone | while | flops 262149 | bytes 1573063 | solution.py:23
  178.9 1.2 bitcast_add_fusion.6
  181.3 1.2 bitcast_add_fusion.6
  183.8 1.2 bitcast_add_fusion.6
  186.3 1.2 bitcast_add_fusion.6
  191.3 13.1 %while.89 = (s32[]{:T(128)}, f32[8,128,128]{2,1,0:T(8,128)S(1)}, f32[8,128]{1,0:T(8,128)S(1)}, f32[128,128]{1,0:T(8,128)S(1)}, f32[8,128]{1,0:T(8,128)S(1)}, /*i...) while((s32[]{:T(128)}, f32[8,128,128]{2,1,0:T(8,128)S(1)}, ...), condition=%wide.region_6.7_spmd.clone.clone, body=%wide.region_5.6_spmd.clone.sunk.clone | while | flops 8585218 | bytes 399477 | solution.py:165
  204.7 18.2 %all-gather.4 = f32[16,1,128]{2,1,0:T(1,128)S(1)} all-gather(f32[1,1,128]{2,1,0:T(1,128)S(1)} %bitcast.334), channel_id=4, replica_groups=mesh['seq'=32,'head'=16] {'head'}, dimensions={0}, use_global_device_ids=true | all-gather | bytes 8704 | tf_op jit(solution)/shard_map/all_gather | solution.py:316
  223.3 23.8 %psum.14 = f32[128]{0:T(128)S(1)} all-reduce(f32[128]{0:T(128)S(1)} %multiply_reduce_fusion.3), channel_id=1, replica_groups=mesh['seq'=32,'head'=16] {'head'}, use_global_device_ids=true, to_apply=%region_10.11 | all-reduce | flops 128 | bytes 1024 | tf_op jit(solution)/shard_map/psum | solution.py:320
  248.3 2.3 while.87
  251.7 157.9 %all-gather.10.cloned.1.call-done = f32[256,128,128]{2,1,0:T(8,128)} async-done(((f32[8,128,128]{2,1,0:T(8,128)}), f32[256,128,128]{2,1,0:T(8,128)}) %all-gather.10.cloned.1.call-update) | async-done | bytes 16777232 | tf_op jit(solution)/shard_map/all_gather | solution.py:14
  409.6 19.7 %while.88 = (s32[]{:T(128)}, f32[8,128,128]{2,1,0:T(8,128)S(1)}, s32[]{:T(128)}, f32[32,8,1,1]{1,3,2,0:T(1,128)S(1)}, f32[32,8,128,128]{3,2,1,0:T(8,128)}) while((s32[]{:T(128)}, f32[8,128,128]{2,1,0:T(8,128)S(1)}, s32[]{:T(128)}, f32[32,8,1,1]{1,3,2,0:T(1,128)S(1)}, f32[32,8,128,128]{3,2,1,0:T(8,128)}) %tuple.222), condition=%wide.region_14.15_spmd.clone, body=%wide.region_13.14_spmd.sunk.clone | while | flops 262150 | bytes 1573075 | solution.py:23
  430.2 112.0 %while.90 = (s32[]{:T(128)}, f32[128,128]{1,0:T(8,128)S(1)}, f32[128,128]{1,0:T(8,128)S(1)}, f32[128,128]{0,1:T(8,128)S(1)}, f32[8,128,128]{2,1,0:T(8,128)S(1)},...) while((s32[]{:T(128)}, f32[128,128]{1,0:T(8,128)S(1)}, ...), condition=%wide.region_24.25_spmd.clone.clone, body=%wide.region_15.24_spmd.clone.sunk.clone | while | flops 25854976 | bytes 1473321 | solution.py:238
  431.7 1.3 multiply_reduce_fusion.9
  437.0 1.3 dynamic_slice.354
  438.3 1.3 add_bitcast_fusion.3
  439.6 1.3 dynamic_update_slice.44
  440.9 1.2 dynamic_slice.353
  445.7 1.3 multiply_reduce_fusion.9
  451.0 1.3 dynamic_slice.354
  452.3 1.3 add_bitcast_fusion.3
  453.6 1.3 dynamic_update_slice.44
  454.9 1.2 dynamic_slice.353
  459.7 1.3 multiply_reduce_fusion.9
  465.0 1.3 dynamic_slice.354
  466.3 1.3 add_bitcast_fusion.3
  467.6 1.3 dynamic_update_slice.44
  468.9 1.2 dynamic_slice.353
  473.7 1.3 multiply_reduce_fusion.9
  479.0 1.3 dynamic_slice.354
  480.3 1.3 add_bitcast_fusion.3
  481.6 1.3 dynamic_update_slice.44
  482.9 1.2 dynamic_slice.353
  487.7 1.3 multiply_reduce_fusion.9
  493.0 1.3 dynamic_slice.354
  494.3 1.3 add_bitcast_fusion.3
  495.6 1.3 dynamic_update_slice.44
  496.9 1.2 dynamic_slice.353
  501.7 1.3 multiply_reduce_fusion.9
  507.0 1.3 dynamic_slice.354
  508.3 1.3 add_bitcast_fusion.3
  509.6 1.3 dynamic_update_slice.44
  510.9 1.2 dynamic_slice.353
  515.7 1.3 multiply_reduce_fusion.9
  521.0 1.3 dynamic_slice.354
  522.3 1.3 add_bitcast_fusion.3
  523.6 1.3 dynamic_update_slice.44
  524.9 1.2 dynamic_slice.353
  529.7 1.3 multiply_reduce_fusion.9
  535.0 1.3 dynamic_slice.354
  536.3 1.3 add_bitcast_fusion.3
  537.6 1.3 dynamic_update_slice.44
  538.9 1.2 dynamic_slice.353
  543.6 4.3 collective-permute-start.2
  547.9 1.4 divide_multiply_fusion
  549.3 3.3 collective-permute-done.2
  553.5 118.1 %all-reduce.3.cloned.1.call-done = f32[2,128,128]{2,1,0:T(8,128)} async-done(((f32[2,128,128]{2,1,0:T(8,128)}), f32[2,128,128]{2,1,0:T(8,128)}) %all-reduce.3.cloned.1.call-update) | async-done | bytes 131088 | tf_op jit(solution)/shard_map/psum | solution.py:345
  672.7 2.8 collective-permute-start.3
  675.4 6.0 collective-permute-done.3
  (341 shorter events, 111.0 us)
Async XLA Ops:
  7.2 184.1 %copy-start.7 = (f32[8]{0:T(128)S(1)}, f32[8]{0:T(128)}, u32[]{:S(2)}) copy-start(f32[8]{0:T(128)} %param.31) | copy-start | bytes 100
  7.2 197.3 %copy-start = (bf16[128,1024]{1,0:T(8,128)(2,1)S(1)}, bf16[128,1024]{1,0:T(8,128)(2,1)}, u32[]{:S(2)}) copy-start(bf16[128,1024]{1,0:T(8,128)(2,1)} %param.26) | copy-start | bytes 786436
  7.2 215.8 %copy-start.4 = (f32[1024]{0:T(1024)S(1)}, f32[1024]{0:T(1024)}, u32[]{:S(2)}) copy-start(f32[1024]{0:T(1024)} %param.34) | copy-start | bytes 12292
  7.2 215.8 %copy-start.3 = (bf16[128,1024]{1,0:T(8,128)(2,1)S(1)}, bf16[128,1024]{1,0:T(8,128)(2,1)}, u32[]{:S(2)}) copy-start(bf16[128,1024]{1,0:T(8,128)(2,1)} %param.35) | copy-start | bytes 786436
  7.2 165.4 %all-gather.8.cloned.1.call-start = ((), (), s32[]{:S(2)}) async-start(), calls=%async_computation.1 | async-start | bytes 17301504 | tf_op jit(solution)/shard_map/all_gather | solution.py:14
  8.0 12.5 %collective-permute-start = (bf16[2,3,128]{2,1,0:T(4,128)(2,1)S(1)}, bf16[2,3,128]{2,1,0:T(4,128)(2,1)S(1)}, u32[]{:S(2)}, u32[]{:S(2)}) collective-permute-start(bf16[2,3,128]{2,1,0:T(4,128)(2,1)S(1)} %slice.125), channel_id=1, source_target_pairs={{0,16},{16,32},{32,48},{48,64},{64,80},{80,96},{96,112},{112,128},... | collective-permute-start | bytes 4616 | tf_op jit(solution)/shard_map/ppermute | solution.py:29
  13.3 8.7 %collective-permute-start.1 = (bf16[3,1024]{1,0:T(4,128)(2,1)S(1)}, bf16[3,1024]{1,0:T(4,128)(2,1)S(1)}, u32[]{:S(2)}, u32[]{:S(2)}) collective-permute-start(bf16[3,1024]{1,0:T(4,128)(2,1)S(1)} %slice.135), channel_id=1, source_target_pairs={{0,16},{16,32},{32,48},{48,64},{64,80},{80,96},{96,112},{112,128},... | collective-permute-start | bytes 18440 | tf_op jit(solution)/shard_map/ppermute | solution.py:29
  18.3 0.8 copy-start.6
  25.9 0.8 copy-start.1
  26.7 382.9 %all-gather.10.cloned.1.call-start = ((), (), s32[]{:S(2)}) async-start(), calls=%async_computation.2 | async-start | bytes 17301504 | tf_op jit(solution)/shard_map/all_gather | solution.py:14
  191.2 356.7 %copy-start.5 = (f32[8,128]{1,0:T(8,128)S(1)}, f32[8,128]{1,0:T(8,128)}, u32[]{:S(2)}) copy-start(f32[8,128]{1,0:T(8,128)} %param.28) | copy-start | bytes 12292
  250.7 0.8 copy-start.2
  251.5 420.1 %all-reduce.3.cloned.1.call-start = ((), (), s32[]{:S(2)}) async-start(), calls=%async_computation | async-start | bytes 262144 | tf_op jit(solution)/shard_map/psum | solution.py:345
  543.6 9.0 %collective-permute-start.2 = (f32[3,1024]{1,0:T(4,128)S(1)}, f32[3,1024]{1,0:T(4,128)S(1)}, u32[]{:S(2)}, u32[]{:S(2)}) collective-permute-start(f32[3,1024]{1,0:T(4,128)S(1)} %slice.164), channel_id=1, source_target_pairs={{16,0},{32,16},{48,32},{64,48},{80,64},{96,80},{112,96},{128,112},... | collective-permute-start | bytes 36872 | tf_op jit(solution)/shard_map/ppermute | solution.py:29
  672.7 8.8 %collective-permute-start.3 = (f32[2,3,128]{2,1,0:T(4,128)S(1)}, f32[2,3,128]{2,1,0:T(4,128)S(1)}, u32[]{:S(2)}, u32[]{:S(2)}) collective-permute-start(f32[2,3,128]{2,1,0:T(4,128)S(1)} %slice.169), channel_id=1, source_target_pairs={{16,0},{32,16},{48,32},{64,48},{80,64},{96,80},{112,96},{128,112},... | collective-permute-start | bytes 9224 | tf_op jit(solution)/shard_map/ppermute | solution.py:29
Sparse Core Ops, SparseCore 0:
  26.8 145.7 all-gather.7
  251.6 157.9 all-gather.9
  543.5 128.0 all-reduce.2
